TPU v7x, 32 devices: a whole 2x2x4 slice. The times are simulated.
32 devices in a mesh: dp: 8 (over z, y), seq: 4 (over x, core).
Axes of the slice: x: 2, y: 2, z: 4, core: 2. Of those that a mesh axis runs over, the one named last changes fastest.
Arguments:
- hidden_in: bfloat16 [32, 1024, 768], P('dp', 'seq'), may hold values from -6 to 6
- time_table: bfloat16 [1024, 128], replicated, may hold values from -6 to 6
- time_step: int32 [32], P('dp'), may hold values from 0 to 1023
- token_pos: int32 [32, 1024], P('dp', 'seq'), may hold values from 0 to 3071, as said below
- heads_weight: bfloat16 [768, 2304], P('seq'), may hold values from -0.15625 to 0.15625
- merge_weight: bfloat16 [768, 768], P('seq'), may hold values from -1.75 to 1.75
- lift_weight: bfloat16 [768, 3072], P('seq'), may hold values from -0.21875 to 0.21875
- lift_bias: bfloat16 [3072], P('seq'), may hold values from -3 to 3
- drop_weight: bfloat16 [3072, 768], P('seq'), may hold values from -0.109375 to 0.109375
- drop_bias: bfloat16 [768], P('seq'), may hold values from -3 to 3
- modulate_weight: bfloat16 [4608, 128], P('seq'), may hold values from -0.5 to 0.5
- modulate_bias: bfloat16 [4608], P('seq'), may hold values from -3 to 3
- first_gain: bfloat16 [768], P('seq'), may hold values from 0.099609375 to 1.8984375
- second_gain: bfloat16 [768], P('seq'), may hold values from 0.099609375 to 1.8984375
- out_grad: bfloat16 [32, 1024, 768], P('dp', 'seq'), may hold values from -6 to 6
Outputs:
- block_out: bfloat16 [32, 1024, 768], P('dp', 'seq')
- input_grad: bfloat16 [32, 1024, 768], P('dp', 'seq')
- heads_grad: float32 [768, 2304], P('seq')
- merge_grad: float32 [768, 768], P('seq')
- lift_grad: float32 [768, 3072], P('seq')
- liftbias_grad: float32 [3072], P('seq')
- drop_grad: float32 [3072, 768], P('seq')
- dropbias_grad: float32 [768], P('seq')
- modulate_grad: float32 [4608, 128], P('seq')
- modulatebias_grad: float32 [4608], P('seq')
- firstgain_grad: float32 [768], P('seq')
- secondgain_grad: float32 [768], P('seq')
- table_grad: float32 [1024, 128], P('seq')
Inputs may be any that keep to these rules, and one draw needn't show every extreme that they name: `token_pos`: positions count up by one along a row and start again at 0 at each separator token; in every aligned group of 4 rows one row holds no separator; such a row in the first group starts at 2048, such a row in the second group starts at 0.
All inputs are finite; a program needn't handle non-finite values.
Results may differ from a plain program's by a relative error of at most 0.017.
The roundings to bfloat16 on the way count: a program that leaves them out, or rounds other values in their place, can miss the bound.
Values may be sent and summed in bfloat16 or wider, within the bound.
No kernel may reach another device: no remote copies, remote signals or barrier semaphores. Data moves between devices by JAX's collectives and lax.ppermute only.
A program may use at most 320 MiB of HBM per device.

v0:
```python
from functools import partial
import math
import jax
import jax.numpy as jnp
from jax import lax
from jax.sharding import PartitionSpec as P

HEADS = 12
EPSILON = 1e-05


def rotate_half(values):
    middle = values.shape[-1] // 2
    return jnp.concatenate([-values[..., middle:], values[..., :middle]], axis=-1)


def rotate(values, cosine, sine):
    return values * cosine + rotate_half(values) * sine


def unrotate(values, cosine, sine):
    return values * cosine - rotate_half(values * sine)


def norm_forward(values, gain):
    center = values - jnp.mean(values, axis=-1, keepdims=True)
    inverse = lax.rsqrt(jnp.mean(center * center, axis=-1, keepdims=True) + EPSILON)
    unit = center * inverse
    return (unit, inverse, unit * gain)


def norm_backward(normed_grad, unit, inverse, gain):
    unit_grad = normed_grad * gain
    first = jnp.mean(unit_grad, axis=-1, keepdims=True)
    second = jnp.mean(unit_grad * unit, axis=-1, keepdims=True)
    return inverse * (unit_grad - first - unit * second)


def grouping(seqs, span):
    group = 1
    while group * span < 512 and seqs % (group * 2) == 0:
        group = group * 2
    return group


def shards(
    hidden_in,
    time_table,
    time_step,
    token_pos,
    heads_weight,
    merge_weight,
    lift_weight,
    lift_bias,
    drop_weight,
    drop_bias,
    modulate_weight,
    modulate_bias,
    first_gain,
    second_gain,
    out_grad,
):
    float_type = jnp.float32
    low_type = jnp.bfloat16
    position_count = lax.axis_size("seq")
    hidden_rows, upstream_rows, places_rows = (hidden_in, out_grad, token_pos)
    seqs, span, width = hidden_rows.shape
    length = span * position_count
    head_width = width // HEADS
    scale = 1.0 / math.sqrt(head_width)
    gathered = (
        lax.all_gather(heads_weight, "seq", axis=0, tiled=True),
        lax.all_gather(merge_weight, "seq", axis=0, tiled=True),
        lax.all_gather(lift_weight, "seq", axis=0, tiled=True),
        lax.all_gather(lift_bias, "seq", axis=0, tiled=True),
        lax.all_gather(drop_weight, "seq", axis=0, tiled=True),
        lax.all_gather(drop_bias, "seq", axis=0, tiled=True),
        lax.all_gather(modulate_weight, "seq", axis=0, tiled=True),
        lax.all_gather(modulate_bias, "seq", axis=0, tiled=True),
        lax.all_gather(first_gain, "seq", axis=0, tiled=True),
        lax.all_gather(second_gain, "seq", axis=0, tiled=True),
    )
    w_heads, w_merge, w_lift, b_lift, w_drop, b_drop, w_mod, b_mod, gain_one, gain_two = gathered
    gain_one = gain_one.astype(float_type)
    gain_two = gain_two.astype(float_type)
    table_rows = time_table.shape[0]
    choose = (time_step[:, None] == jnp.arange(table_rows, dtype=jnp.int32)[None, :]).astype(
        low_type
    )
    conds = jnp.dot(choose, time_table, preferred_element_type=float_type)
    modulation = lax.dot_general(
        conds.astype(low_type), w_mod, (((1,), (1,)), ((), ())), preferred_element_type=float_type
    ) + b_mod.astype(float_type)
    pieces = [piece[:, None, :] for piece in jnp.split(modulation, 6, axis=-1)]
    shift_a, scale_a, gate_a, shift_b, scale_b, gate_b = pieces
    positions = places_rows.astype(float_type)
    freqs = 10000.0 ** (-jnp.arange(0, head_width, 2, dtype=float_type) / head_width)
    angles = positions[..., None] * freqs
    angles = jnp.concatenate([angles, angles], axis=-1)
    cosine = jnp.cos(angles)[:, :, None, :]
    sine = jnp.sin(angles)[:, :, None, :]
    head_layout = (seqs, span, HEADS, head_width)
    inputs = hidden_rows.astype(float_type)
    unit_one, inverse_one, normed_one = norm_forward(inputs, gain_one)
    adapted_one = (normed_one * (1.0 + scale_a) + shift_a).astype(low_type)
    projected = jnp.einsum("scd,de->sce", adapted_one, w_heads, preferred_element_type=float_type)
    query_raw, key_raw, value_raw = jnp.split(projected, 3, axis=-1)
    query = rotate(query_raw.reshape(head_layout), cosine, sine).astype(low_type)
    keys_local = (
        rotate(key_raw.reshape(head_layout), cosine, sine)
        .astype(low_type)
        .reshape(seqs, span, width)
    )
    values_local = value_raw.astype(low_type)
    keys_all, values_all = (
        lax.all_gather(keys_local, "seq", axis=1, tiled=True),
        lax.all_gather(values_local, "seq", axis=1, tiled=True),
    )
    group = grouping(seqs, span)
    blocks = seqs // group

    def split_groups(array):
        return array.reshape((blocks, group) + array.shape[1:])

    def attend(block):
        query_b, keys_b, values_b = block
        keys_h = keys_b.reshape(group, length, HEADS, head_width)
        values_h = values_b.reshape(group, length, HEADS, head_width)
        scores = (
            jnp.einsum("gqhd,gkhd->ghqk", query_b, keys_h, preferred_element_type=float_type)
            * scale
        )
        peak = jnp.max(scores, axis=-1, keepdims=True)
        expos = jnp.exp(scores - peak)
        totals = jnp.sum(expos, axis=-1, keepdims=True)
        probs = (expos / totals).astype(low_type)
        mixed_b = jnp.einsum("ghqk,gkhd->gqhd", probs, values_h, preferred_element_type=float_type)
        return (mixed_b, peak[..., 0] + jnp.log(totals[..., 0]))

    mixed, logsum = lax.map(
        attend, (split_groups(query), split_groups(keys_all), split_groups(values_all))
    )
    mixed_low = mixed.reshape(seqs, span, width).astype(low_type)
    branch = jnp.einsum("scd,de->sce", mixed_low, w_merge, preferred_element_type=float_type)
    middle = inputs + gate_a * branch
    unit_two, inverse_two, normed_two = norm_forward(middle, gain_two)
    adapted_two = (normed_two * (1.0 + scale_b) + shift_b).astype(low_type)
    upper = jnp.einsum(
        "scd,df->scf", adapted_two, w_lift, preferred_element_type=float_type
    ) + b_lift.astype(float_type)
    active, gelu_back = jax.vjp(partial(jax.nn.gelu, approximate=True), upper)
    active_low = active.astype(low_type)
    lowered = jnp.einsum(
        "scf,fd->scd", active_low, w_drop, preferred_element_type=float_type
    ) + b_drop.astype(float_type)
    block_out = (middle + gate_b * lowered).astype(low_type)
    upstream = upstream_rows.astype(float_type)
    gate_b_grad = jnp.sum(upstream * lowered, axis=1)
    lowered_grad = (gate_b * upstream).astype(low_type)
    drop_grad = jnp.einsum(
        "scf,scd->fd", active_low, lowered_grad, preferred_element_type=float_type
    )
    dropbias_grad = jnp.sum(lowered_grad.astype(float_type), axis=(0, 1))
    active_grad = jnp.einsum("scd,fd->scf", lowered_grad, w_drop, preferred_element_type=float_type)
    (upper_grad,) = gelu_back(active_grad)
    upper_low = upper_grad.astype(low_type)
    lift_grad = jnp.einsum("scd,scf->df", adapted_two, upper_low, preferred_element_type=float_type)
    liftbias_grad = jnp.sum(upper_low.astype(float_type), axis=(0, 1))
    adapted_two_grad = jnp.einsum(
        "scf,df->scd", upper_low, w_lift, preferred_element_type=float_type
    )
    shift_b_grad = jnp.sum(adapted_two_grad, axis=1)
    scale_b_grad = jnp.sum(adapted_two_grad * normed_two, axis=1)
    normed_two_grad = adapted_two_grad * (1.0 + scale_b)
    secondgain_grad = jnp.sum(normed_two_grad * unit_two, axis=(0, 1))
    middle_grad = upstream + norm_backward(normed_two_grad, unit_two, inverse_two, gain_two)
    gate_a_grad = jnp.sum(middle_grad * branch, axis=1)
    branch_grad = (gate_a * middle_grad).astype(low_type)
    merge_grad = jnp.einsum(
        "scd,sce->de", mixed_low, branch_grad, preferred_element_type=float_type
    )
    mixed_grad = jnp.einsum(
        "sce,de->scd", branch_grad, w_merge, preferred_element_type=float_type
    ).astype(low_type)
    keys_back, values_back = (
        lax.all_gather(keys_local, "seq", axis=1, tiled=True),
        lax.all_gather(values_local, "seq", axis=1, tiled=True),
    )

    def attend_back(block):
        query_b, keys_b, values_b, logsum_b, mixed_grad_b = block
        keys_h = keys_b.reshape(group, length, HEADS, head_width)
        values_h = values_b.reshape(group, length, HEADS, head_width)
        scores = (
            jnp.einsum("gqhd,gkhd->ghqk", query_b, keys_h, preferred_element_type=float_type)
            * scale
        )
        probs = jnp.exp(scores - logsum_b[..., None])
        probs_low = probs.astype(low_type)
        values_term = jnp.einsum(
            "ghqk,gqhd->gkhd", probs_low, mixed_grad_b, preferred_element_type=float_type
        )
        probs_grad = jnp.einsum(
            "gqhd,gkhd->ghqk", mixed_grad_b, values_h, preferred_element_type=float_type
        )
        center = jnp.sum(probs * probs_grad, axis=-1, keepdims=True)
        scores_grad = (probs * (probs_grad - center)).astype(low_type)
        query_term = (
            jnp.einsum("ghqk,gkhd->gqhd", scores_grad, keys_h, preferred_element_type=float_type)
            * scale
        )
        keys_term = (
            jnp.einsum("ghqk,gqhd->gkhd", scores_grad, query_b, preferred_element_type=float_type)
            * scale
        )
        return (
            query_term,
            keys_term.reshape(group, length, width),
            values_term.reshape(group, length, width),
        )

    mixed_grad_h = mixed_grad.reshape(head_layout)
    query_term, keys_term, values_term = lax.map(
        attend_back,
        (
            split_groups(query),
            split_groups(keys_back),
            split_groups(values_back),
            logsum,
            split_groups(mixed_grad_h),
        ),
    )
    keys_grad, values_grad = (
        lax.psum_scatter(
            keys_term.reshape(seqs, length, width).astype(jnp.bfloat16),
            "seq",
            scatter_dimension=1,
            tiled=True,
        ).astype(jnp.float32),
        lax.psum_scatter(
            values_term.reshape(seqs, length, width).astype(jnp.bfloat16),
            "seq",
            scatter_dimension=1,
            tiled=True,
        ).astype(jnp.float32),
    )
    query_grad = unrotate(query_term.reshape(head_layout), cosine, sine).reshape(seqs, span, width)
    key_grad = unrotate(keys_grad.reshape(head_layout), cosine, sine).reshape(seqs, span, width)
    projected_grad = jnp.concatenate([query_grad, key_grad, values_grad], axis=-1).astype(low_type)
    heads_grad = jnp.einsum(
        "scd,sce->de", adapted_one, projected_grad, preferred_element_type=float_type
    )
    adapted_one_grad = jnp.einsum(
        "sce,de->scd", projected_grad, w_heads, preferred_element_type=float_type
    )
    shift_a_grad = jnp.sum(adapted_one_grad, axis=1)
    scale_a_grad = jnp.sum(adapted_one_grad * normed_one, axis=1)
    normed_one_grad = adapted_one_grad * (1.0 + scale_a)
    firstgain_grad = jnp.sum(normed_one_grad * unit_one, axis=(0, 1))
    input_grad = (
        middle_grad + norm_backward(normed_one_grad, unit_one, inverse_one, gain_one)
    ).astype(low_type)
    modulation_grad = jnp.concatenate(
        [shift_a_grad, scale_a_grad, gate_a_grad, shift_b_grad, scale_b_grad, gate_b_grad], axis=-1
    )
    modulate_grad = jnp.einsum("sm,sc->mc", modulation_grad, conds, precision=lax.Precision.HIGHEST)
    modulatebias_grad = jnp.sum(modulation_grad, axis=0)
    conds_grad = jnp.einsum(
        "sm,mc->sc", modulation_grad, w_mod.astype(float_type), precision=lax.Precision.HIGHEST
    )
    table_grad = jnp.einsum(
        "sn,sc->nc", choose.astype(float_type), conds_grad, precision=lax.Precision.HIGHEST
    )
    terms = (
        heads_grad,
        merge_grad,
        lift_grad,
        liftbias_grad,
        drop_grad,
        dropbias_grad,
        modulate_grad,
        modulatebias_grad,
        firstgain_grad,
        secondgain_grad,
        table_grad,
    )
    shares = (
        lax.psum_scatter(
            terms[0].astype(jnp.bfloat16), "seq", scatter_dimension=0, tiled=True
        ).astype(jnp.float32),
        lax.psum_scatter(
            terms[1].astype(jnp.bfloat16), "seq", scatter_dimension=0, tiled=True
        ).astype(jnp.float32),
        lax.psum_scatter(
            terms[2].astype(jnp.bfloat16), "seq", scatter_dimension=0, tiled=True
        ).astype(jnp.float32),
        lax.psum_scatter(
            terms[3].astype(jnp.bfloat16), "seq", scatter_dimension=0, tiled=True
        ).astype(jnp.float32),
        lax.psum_scatter(
            terms[4].astype(jnp.bfloat16), "seq", scatter_dimension=0, tiled=True
        ).astype(jnp.float32),
        lax.psum_scatter(
            terms[5].astype(jnp.bfloat16), "seq", scatter_dimension=0, tiled=True
        ).astype(jnp.float32),
        lax.psum_scatter(
            terms[6].astype(jnp.bfloat16), "seq", scatter_dimension=0, tiled=True
        ).astype(jnp.float32),
        lax.psum_scatter(
            terms[7].astype(jnp.bfloat16), "seq", scatter_dimension=0, tiled=True
        ).astype(jnp.float32),
        lax.psum_scatter(
            terms[8].astype(jnp.bfloat16), "seq", scatter_dimension=0, tiled=True
        ).astype(jnp.float32),
        lax.psum_scatter(
            terms[9].astype(jnp.bfloat16), "seq", scatter_dimension=0, tiled=True
        ).astype(jnp.float32),
        lax.psum_scatter(
            terms[10].astype(jnp.bfloat16), "seq", scatter_dimension=0, tiled=True
        ).astype(jnp.float32),
    )
    summed = lax.psum(
        (
            shares[0],
            shares[1],
            shares[2],
            shares[3],
            shares[4],
            shares[5],
            shares[6],
            shares[7],
            shares[8],
            shares[9],
            shares[10],
        ),
        "dp",
    )
    return (
        block_out,
        input_grad,
        summed[0],
        summed[1],
        summed[2],
        summed[3],
        summed[4],
        summed[5],
        summed[6],
        summed[7],
        summed[8],
        summed[9],
        summed[10],
    )


def solution(mesh):
    return jax.shard_map(
        shards,
        mesh=mesh,
        in_specs=(
            P("dp", "seq", None),
            P(),
            P("dp"),
            P("dp", "seq"),
            P("seq", None),
            P("seq", None),
            P("seq", None),
            P("seq"),
            P("seq", None),
            P("seq"),
            P("seq", None),
            P("seq"),
            P("seq"),
            P("seq"),
            P("dp", "seq", None),
        ),
        out_specs=(
            P("dp", "seq", None),
            P("dp", "seq", None),
            P("seq", None),
            P("seq", None),
            P("seq", None),
            P("seq"),
            P("seq", None),
            P("seq"),
            P("seq", None),
            P("seq"),
            P("seq"),
            P("seq"),
            P("seq", None),
        ),
        check_vma=False,
    )
```

profile of v0, /device:TPU:0, one launch (start us, length us, event | category | flops | bytes accessed | tf_op | source)
XLA Modules:
  0.0 1162.3 jit_solution(14610913163980127939)
XLA Ops:
  13.3 8.5 all-reduce.10
  33.2 29.1 %all-gather.12.cloned.1.call-done = bf16[768,2304]{1,0:T(8,128)(2,1)} async-done(((bf16[192,2304]{1,0:T(8,128)(2,1)}), bf16[768,2304]{1,0:T(8,128)(2,1)}) %all-gather.12.cloned.1.call-update) | async-done | bytes 3538960 | tf_op jit(solution)/shard_map/all_gather | solution.py:72
  62.3 6.2 fusion.52
  96.0 6.6 add_convert_fusion.2
  107.2 5.6 all-gather.1
  121.9 8.7 copy.93
  130.6 37.9 %all-gather.16.cloned.1.call-done = bf16[4,1024,768]{2,1,0:T(8,128)(2,1)} async-done(((bf16[4,256,768]{2,1,0:T(8,128)(2,1)}), bf16[4,1024,768]{2,1,0:T(8,128)(2,1)}) %all-gather.16.cloned.1.call-update) | async-done | bytes 6291472 | tf_op jit(solution)/shard_map/all_gather | solution.py:116
  168.5 8.7 copy.94
  177.2 74.9 %while.28 = (s32[]{:T(128)}, bf16[2,2,256,12,64]{2,4,3,1,0:T(8,128)(2,1)}, f32[2,2,12,256]{3,2,1,0:T(8,128)S(1)}, bf16[2,2,1024,768]{2,3,1,0:T(8,128)(2,1)}, bf1...) while((s32[]{:T(128)}, bf16[2,2,256,12,64]{2,4,3,1,0:T(8,128)(2,1)}, ...), condition=%wide.region_5.6_spmd.clone, body=%wide.region_2.5_spmd.sunk.clone | while | flops 1667229696 | bytes 96952408 | solution.py:140
  180.9 10.2 multiply_reduce_fusion.11
  191.1 11.7 %fusion.143 = f32[2,12,256]{2,1,0:T(8,128)S(1)} fusion(f32[2,12,256,1024]{3,2,1,0:T(8,128)} %get-tuple-element.385, f32[2,12,256]{2,1,0:T(8,128)S(1)} %get-tuple-element.386), kind=kLoop, calls=%fused_computation.3.clone.1.clone | loop fusion | flops 18868224 | bytes 25214976 | tf_op jit(solution)/shard_map/while/body/eval_jaxpr/reduce_sum | solution.py:135
  202.8 11.8 %bitcast_dynamic-update-slice_fusion.9 = bf16[2,2,256,12,64]{2,4,3,1,0:T(8,128)(2,1)} fusion(bf16[2,2,256,12,64]{2,4,3,1,0:T(8,128)(2,1)} %get-tuple-element.425, s32[]{:T(128)S(6)} %copy.125, bf16[2,1024,12,64]{1,3,2,0:T(8,128)(2,1)S(1)} %bitcast.191, f32[2,12,256,1024]{3,2,1,0:T(8,128)} %get-tuple-element.385, ...), kind=kOutput, calls=%fused_computation.5.clone.1.clone | convolution fusion | flops 830472192 | bytes 29933572 | tf_op jit(solution)/shard_map/while/body/eval_jaxpr/ghqk,gkhd->gqhd/dot_general | solution.py:137
  218.3 10.3 multiply_reduce_fusion.11
  228.5 11.8 %fusion.143 = f32[2,12,256]{2,1,0:T(8,128)S(1)} fusion(f32[2,12,256,1024]{3,2,1,0:T(8,128)} %get-tuple-element.385, f32[2,12,256]{2,1,0:T(8,128)S(1)} %get-tuple-element.386), kind=kLoop, calls=%fused_computation.3.clone.1.clone | loop fusion | flops 18868224 | bytes 25214976 | tf_op jit(solution)/shard_map/while/body/eval_jaxpr/reduce_sum | solution.py:135
  240.4 11.8 %bitcast_dynamic-update-slice_fusion.9 = bf16[2,2,256,12,64]{2,4,3,1,0:T(8,128)(2,1)} fusion(bf16[2,2,256,12,64]{2,4,3,1,0:T(8,128)(2,1)} %get-tuple-element.425, s32[]{:T(128)S(6)} %copy.125, bf16[2,1024,12,64]{1,3,2,0:T(8,128)(2,1)S(1)} %bitcast.191, f32[2,12,256,1024]{3,2,1,0:T(8,128)} %get-tuple-element.385, ...), kind=kOutput, calls=%fused_computation.5.clone.1.clone | convolution fusion | flops 830472192 | bytes 29933572 | tf_op jit(solution)/shard_map/while/body/eval_jaxpr/ghqk,gkhd->gqhd/dot_general | solution.py:137
  259.5 11.3 fusion.40
  270.8 16.6 %fusion.93 = (bf16[3072]{0:T(1024)(128)(2,1)}, bf16[4,256,3072]{2,1,0:T(8,128)(2,1)}) fusion(f32[4,256,3072]{2,1,0:T(8,128)} %fusion.40, f32[3072]{0:T(1024)S(1)} %bitcast.210, bf16[3072,768]{1,0:T(8,128)(2,1)} %all-gather.22.cloned.1.call-done, bf16[4,256,768]{2,1,0:T(8,128)(2,1)S(1)} %copy-done.27, f32[4,768]{1,0:T(4,128)S(1)} %copy-done.36), kind=kOutput, calls=%fused_computation.174 | convolution fusion | flops 4903400448 | bytes 25196544 | tf_op jit(solution)/shard_map/scd,fd->scf/dot_general | solution.py:164
  287.4 10.2 multiply_reduce_fusion.2
  297.6 15.1 %fusion.67 = (f32[4,768]{1,0:T(4,128)}, bf16[4,256,768]{2,1,0:T(8,128)(2,1)}, f32[4,768]{1,0:T(4,128)}, f32[4,256,768]{2,1,0:T(8,128)S(1)}) fusion(bf16[4,256,768]{2,1,0:T(8,128)(2,1)S(1)} %copy-done.27, f32[768]{0:T(1024)S(1)} %copy-done.65, f32[4,256,768]{2,1,0:T(8,128)S(1)} %copy-done.18, f32[4,768]{1,0:T(4,128)S(1)} %copy-done.36, ...), kind=kOutput, calls=%fused_computation.96 | convolution fusion | flops 4877445120 | bytes 33114112 | tf_op jit(solution)/shard_map/scf,fd->scd/dot_general | solution.py:153
  317.4 178.6 %while.29 = (s32[]{:T(128)}, f32[2,2,256,12,64]{2,4,3,1,0:T(8,128)}, bf16[2,2,1024,768]{2,3,1,0:T(8,128)(2,1)}, bf16[2,2,1024,768]{2,3,1,0:T(8,128)(2,1)}, bf16[...) while((s32[]{:T(128)}, ...), condition=%wide.region_12.13_spmd.clone, body=%wide.region_10.12_spmd.sunk.clone | while | flops 4105562112 | bytes 316326176 | solution.py:223
  323.3 11.5 fusion.153
  334.8 12.2 %fusion.154 = bf16[2,12,64,1024]{3,2,1,0:T(8,128)(2,1)} fusion(f32[2,12,256,1024]{3,2,1,0:T(8,128)} %fusion.153, f32[2,12,256]{2,1,0:T(8,128)S(1)} %dynamic-slice_bitcast_fusion.3, bf16[2,2,256,12,64]{2,4,3,1,0:T(8,128)(2,1)S(1)} %copy-done.6, s32[]{:T(128)S(6)} %copy.135), kind=kOutput, calls=%fused_computation.18.clone.1.clone | convolution fusion | flops 824180736 | bytes 29130756 | tf_op jit(solution)/shard_map/while/body/eval_jaxpr/ghqk,gqhd->gkhd/dot_general | solution.py:200
  347.0 17.6 %multiply_reduce_fusion.12 = (f32[2,12,256]{2,1,0:T(8,128)S(1)}, f32[2,12,256,1024]{3,2,1,0:T(8,128)}) fusion(f32[2,12,256,1024]{3,2,1,0:T(8,128)} %fusion.153, f32[2,12,256]{2,1,0:T(8,128)S(1)} %dynamic-slice_bitcast_fusion.3, bf16[2,1024,12,64]{1,3,2,0:T(8,128)(2,1)} %bitcast.188, bf16[2,2,256,12,64]{2,4,3,1,0:T(8,128)(2,1)} %get-tuple-element.461, ...), kind=kOutput, calls=%fused_computation.15.clone.1.clone | convolution fusion | flops 830466048 | bytes 54312964 | tf_op jit(solution)/shard_map/while/body/eval_jaxpr/gqhd,gkhd->ghqk/dot_general | solution.py:203
  364.6 21.7 %multiply_convert_fusion.9 = bf16[2,12,256,1024]{3,2,1,0:T(8,128)(2,1)} fusion(f32[2,12,256,1024]{3,2,1,0:T(8,128)} %get-tuple-element.404, f32[2,12,256,1024]{3,2,1,0:T(8,128)} %fusion.153, f32[2,12,256]{2,1,0:T(8,128)S(1)} %get-tuple-element.405, f32[2,12,256]{2,1,0:T(8,128)S(1)} %dynamic-slice_bitcast_fusion.3), kind=kLoop, calls=%fused_computation.14.clone.1.clone | loop fusion | flops 31457280 | bytes 62963712 | tf_op jit(solution)/shard_map/while/body/eval_jaxpr/convert_element_type | solution.py:207
  386.3 8.5 bitcast_dynamic-update-slice_fusion.11
  394.8 8.3 broadcast_multiply_fusion.12
  412.4 11.5 fusion.153
  423.9 12.2 %fusion.154 = bf16[2,12,64,1024]{3,2,1,0:T(8,128)(2,1)} fusion(f32[2,12,256,1024]{3,2,1,0:T(8,128)} %fusion.153, f32[2,12,256]{2,1,0:T(8,128)S(1)} %dynamic-slice_bitcast_fusion.3, bf16[2,2,256,12,64]{2,4,3,1,0:T(8,128)(2,1)S(1)} %copy-done.6, s32[]{:T(128)S(6)} %copy.135), kind=kOutput, calls=%fused_computation.18.clone.1.clone | convolution fusion | flops 824180736 | bytes 29130756 | tf_op jit(solution)/shard_map/while/body/eval_jaxpr/ghqk,gqhd->gkhd/dot_general | solution.py:200
  436.1 17.6 %multiply_reduce_fusion.12 = (f32[2,12,256]{2,1,0:T(8,128)S(1)}, f32[2,12,256,1024]{3,2,1,0:T(8,128)}) fusion(f32[2,12,256,1024]{3,2,1,0:T(8,128)} %fusion.153, f32[2,12,256]{2,1,0:T(8,128)S(1)} %dynamic-slice_bitcast_fusion.3, bf16[2,1024,12,64]{1,3,2,0:T(8,128)(2,1)} %bitcast.188, bf16[2,2,256,12,64]{2,4,3,1,0:T(8,128)(2,1)} %get-tuple-element.461, ...), kind=kOutput, calls=%fused_computation.15.clone.1.clone | convolution fusion | flops 830466048 | bytes 54312964 | tf_op jit(solution)/shard_map/while/body/eval_jaxpr/gqhd,gkhd->ghqk/dot_general | solution.py:203
  453.7 21.7 %multiply_convert_fusion.9 = bf16[2,12,256,1024]{3,2,1,0:T(8,128)(2,1)} fusion(f32[2,12,256,1024]{3,2,1,0:T(8,128)} %get-tuple-element.404, f32[2,12,256,1024]{3,2,1,0:T(8,128)} %fusion.153, f32[2,12,256]{2,1,0:T(8,128)S(1)} %get-tuple-element.405, f32[2,12,256]{2,1,0:T(8,128)S(1)} %dynamic-slice_bitcast_fusion.3), kind=kLoop, calls=%fused_computation.14.clone.1.clone | loop fusion | flops 31457280 | bytes 62963712 | tf_op jit(solution)/shard_map/while/body/eval_jaxpr/convert_element_type | solution.py:207
  475.4 8.5 bitcast_dynamic-update-slice_fusion.11
  483.9 8.3 broadcast_multiply_fusion.12
  496.0 8.7 copy.102
  504.7 8.7 copy.106
  520.0 12.4 %bitcast_convert_fusion = bf16[3072,768]{1,0:T(8,128)(2,1)} fusion(bf16[4,256,768]{2,1,0:T(8,128)(2,1)S(1)} %copy-done.28, f32[4,768]{1,0:T(4,128)S(1)} %copy-done.37, f32[4,256,3072]{2,1,0:T(8,128)} %fusion.40, f32[3072]{0:T(1024)S(1)} %bitcast.212), kind=kOutput, calls=%fused_computation.53 | convolution fusion | flops 4868014080 | bytes 18898944 | tf_op jit(solution)/shard_map/scf,scd->fd/dot_general | solution.py:160
  534.4 10.0 bitcast_convert_fusion.1
  548.7 14.7 %reduce-scatter.9.cloned.1.call-done = bf16[4,256,768]{2,1,0:T(8,128)(2,1)} async-done(((bf16[4,1024,768]{2,1,0:T(8,128)(2,1)}), bf16[4,256,768]{2,1,0:T(8,128)(2,1)}) %reduce-scatter.9.cloned.1.call-update) | async-done | bytes 1572880 | tf_op jit(solution)/shard_map/reduce_scatter | solution.py:234
  582.9 7.0 subtract_convert_fusion.1
  589.9 34.6 %reduce-scatter.11.cloned.1.call-done = bf16[4,256,768]{2,1,0:T(8,128)(2,1)} async-done(((bf16[4,1024,768]{2,1,0:T(8,128)(2,1)}), bf16[4,256,768]{2,1,0:T(8,128)(2,1)}) %reduce-scatter.11.cloned.1.call-update) | async-done | bytes 1572880 | tf_op jit(solution)/shard_map/reduce_scatter | solution.py:240
  624.6 9.1 fusion.64
  641.1 7.9 bitcast_convert_fusion.2
  653.3 50.5 %reduce-scatter.19.cloned.1.call-done = bf16[768,768]{1,0:T(8,128)(2,1)} async-done(((bf16[3072,768]{1,0:T(8,128)(2,1)}), bf16[768,768]{1,0:T(8,128)(2,1)}) %reduce-scatter.19.cloned.1.call-update) | async-done | bytes 1179664 | tf_op jit(solution)/shard_map/reduce_scatter | solution.py:300
  703.8 50.3 %reduce-scatter.17.cloned.1.call-done = bf16[192,3072]{1,0:T(8,128)(2,1)} async-done(((bf16[768,3072]{1,0:T(8,128)(2,1)}), bf16[192,3072]{1,0:T(8,128)(2,1)}) %reduce-scatter.17.cloned.1.call-update) | async-done | bytes 1179664 | tf_op jit(solution)/shard_map/reduce_scatter | solution.py:294
  754.2 10.3 all-reduce.9
  769.3 8.0 reduce-scatter.23.cloned.1.call-done
  777.4 28.7 %reduce-scatter.21.cloned.1.call-done = bf16[1152,128]{1,0:T(8,128)(2,1)} async-done(((bf16[4608,128]{1,0:T(8,128)(2,1)}), bf16[1152,128]{1,0:T(8,128)(2,1)}) %reduce-scatter.21.cloned.1.call-update) | async-done | bytes 294928 | tf_op jit(solution)/shard_map/reduce_scatter | solution.py:306
  806.1 43.0 %reduce-scatter.13.cloned.1.call-done = bf16[192,2304]{1,0:T(8,128)(2,1)} async-done(((bf16[768,2304]{1,0:T(8,128)(2,1)}), bf16[192,2304]{1,0:T(8,128)(2,1)}) %reduce-scatter.13.cloned.1.call-update) | async-done | bytes 884752 | tf_op jit(solution)/shard_map/reduce_scatter | solution.py:288
  849.1 306.4 %all-reduce.12 = (f32[192,2304]{1,0:T(8,128)}, f32[192,768]{1,0:T(8,128)}, f32[192,3072]{1,0:T(8,128)}, f32[768]{0:T(1024)}, f32[768,768]{1,0:T(8,128)}, /*index...) all-reduce(bf16[192,2304]{1,0:T(8,128)(2,1)} %reduce-scatter.13.clo, ...), channel_id=1, replica_groups=mesh['dp'=8,'seq'=4] {'dp'}, use_global_device_ids=true, to_apply=%region_18.19 | all-reduce | flops 1952192 | bytes 11718144 | tf_op jit(solution)/shard_map/psum | solution.py:322
  (292 shorter events, 141.8 us)
Async XLA Ops:
  7.2 22.9 %copy-start = (bf16[1024,128]{1,0:T(8,128)(2,1)S(1)}, bf16[1024,128]{1,0:T(8,128)(2,1)}, u32[]{:S(2)}) copy-start(bf16[1024,128]{1,0:T(8,128)(2,1)} %param.20) | copy-start | bytes 786436
  7.2 22.2 %copy-start.10 = (bf16[4,256,768]{2,1,0:T(8,128)(2,1)S(1)}, bf16[4,256,768]{2,1,0:T(8,128)(2,1)}, u32[]{:S(2)}) copy-start(bf16[4,256,768]{2,1,0:T(8,128)(2,1)} %param.19) | copy-start | bytes 4718596
  7.2 22.9 %copy-start.71 = (s32[4]{0:T(128)S(1)}, s32[4]{0:T(128)}, u32[]{:S(2)}) copy-start(s32[4]{0:T(128)} %param.21) | copy-start | bytes 52
  7.2 23.1 %all-gather.10.cloned.1.call-start = ((), (), s32[]{:S(2)}) async-start(), calls=%async_computation.8 | async-start | bytes 1474560 | tf_op jit(solution)/shard_map/all_gather | solution.py:78
  8.0 54.3 %all-gather.12.cloned.1.call-start = ((), (), s32[]{:S(2)}) async-start(), calls=%async_computation.9 | async-start | bytes 4423680 | tf_op jit(solution)/shard_map/all_gather | solution.py:72
  8.7 113.2 %all-gather.14.cloned.1.call-start = ((), (), s32[]{:S(2)}) async-start(), calls=%async_computation.10 | async-start | bytes 7864320 | tf_op jit(solution)/shard_map/all_gather | solution.py:117
  21.7 46.7 %copy-start.42 = (f32[768]{0:T(1024)}, f32[768]{0:T(1024)S(1)}, u32[]{:S(2)}) copy-start(f32[768]{0:T(1024)S(1)} %convert_element_type.165) | copy-start | bytes 9220
  29.4 39.0 %copy-start.40 = (f32[4,256]{1,0:T(4,128)}, f32[4,256]{1,0:T(4,128)S(1)}, u32[]{:S(2)}) copy-start(f32[4,256]{1,0:T(4,128)S(1)} %broadcast_multiply_fusion.9) | copy-start | bytes 12292
  30.1 38.4 %copy-start.44 = (f32[4,256]{1,0:T(4,128)}, f32[4,256]{1,0:T(4,128)S(1)}, u32[]{:S(2)}) copy-start(f32[4,256]{1,0:T(4,128)S(1)} %add_rsqrt_fusion.1) | copy-start | bytes 12292
  33.2 35.3 %copy-start.34 = (f32[4,768]{1,0:T(4,128)}, f32[4,768]{1,0:T(4,128)S(1)}, u32[]{:S(2)}) copy-start(f32[4,768]{1,0:T(4,128)S(1)} %get-tuple-element.257) | copy-start | bytes 36868
  33.2 35.3 %copy-start.48 = (f32[4,768]{1,0:T(4,128)}, f32[4,768]{1,0:T(4,128)S(1)}, u32[]{:S(2)}) copy-start(f32[4,768]{1,0:T(4,128)S(1)} %get-tuple-element.256) | copy-start | bytes 36868
  73.5 95.0 %all-gather.16.cloned.1.call-start = ((), (), s32[]{:S(2)}) async-start(), calls=%async_computation.11 | async-start | bytes 7864320 | tf_op jit(solution)/shard_map/all_gather | solution.py:116
  74.6 15.8 %copy-start.24 = (f32[4,256,64]{1,2,0:T(8,128)}, f32[4,256,64]{1,2,0:T(8,128)S(1)}, u32[]{:S(2)}) copy-start(f32[4,256,64]{1,2,0:T(8,128)S(1)} %get-tuple-element.250) | copy-start | bytes 786436
  79.2 16.8 %copy-start.8 = (f32[4,256,768]{2,1,0:T(8,128)}, f32[4,256,768]{2,1,0:T(8,128)S(1)}, u32[]{:S(2)}) copy-start(f32[4,256,768]{2,1,0:T(8,128)S(1)} %copy.90) | copy-start | bytes 9437188
  102.7 149.5 %all-gather.18.cloned.1.call-start = ((), (), s32[]{:S(2)}) async-start(), calls=%async_computation.12 | async-start | bytes 1474560 | tf_op jit(solution)/shard_map/all_gather | solution.py:73
  103.3 156.1 %all-gather.20.cloned.1.call-start = ((), (), s32[]{:S(2)}) async-start(), calls=%async_computation.13 | async-start | bytes 5898240 | tf_op jit(solution)/shard_map/all_gather | solution.py:74
  103.8 166.9 %all-gather.22.cloned.1.call-start = ((), (), s32[]{:S(2)}) async-start(), calls=%async_computation.14 | async-start | bytes 5898240 | tf_op jit(solution)/shard_map/all_gather | solution.py:76
  104.6 458.9 %reduce-scatter.9.cloned.1.call-start = ((), (), s32[]{:S(2)}) async-start(), calls=%async_computation.15 | async-start | bytes 7864320 | tf_op jit(solution)/shard_map/reduce_scatter | solution.py:234
  177.2 75.0 %copy-start.11 = (bf16[4,256,768]{2,1,0:T(8,128)(2,1)S(1)}, bf16[4,256,768]{2,1,0:T(8,128)(2,1)}, u32[]{:S(2)}) copy-start(bf16[4,256,768]{2,1,0:T(8,128)(2,1)} %param.19) | copy-start | bytes 4718596
  177.2 75.0 %copy-start.38 = (f32[4,768]{1,0:T(4,128)S(1)}, f32[4,768]{1,0:T(4,128)}, u32[]{:S(2)}) copy-start(f32[4,768]{1,0:T(4,128)} %get-tuple-element.258) | copy-start | bytes 36868
  257.3 40.3 %copy-start.46 = (f32[4,256]{1,0:T(4,128)}, f32[4,256]{1,0:T(4,128)S(1)}, u32[]{:S(2)}) copy-start(f32[4,256]{1,0:T(4,128)S(1)} %broadcast_multiply_fusion.8) | copy-start | bytes 12292
  259.4 38.2 %copy-start.67 = (f32[4,256]{1,0:T(4,128)}, f32[4,256]{1,0:T(4,128)S(1)}, u32[]{:S(2)}) copy-start(f32[4,256]{1,0:T(4,128)S(1)} %add_rsqrt_fusion) | copy-start | bytes 12292
  259.4 11.3 copy-start.27
  270.8 16.6 %copy-start.18 = (f32[4,256,768]{2,1,0:T(8,128)S(1)}, f32[4,256,768]{2,1,0:T(8,128)}, u32[]{:S(2)}) copy-start(f32[4,256,768]{2,1,0:T(8,128)} %copy-done.17) | copy-start | bytes 9437188
  270.8 16.6 %copy-start.73 = (bf16[768,3072]{1,0:T(8,128)(2,1)S(1)}, bf16[768,3072]{1,0:T(8,128)(2,1)}, u32[]{:S(2)}) copy-start(bf16[768,3072]{1,0:T(8,128)(2,1)} %all-gather.20.cloned.1.call-done) | copy-start | bytes 14155780
  297.6 16.7 %copy-start.31 = (bf16[768,768]{1,0:T(8,128)(2,1)S(1)}, bf16[768,768]{1,0:T(8,128)(2,1)}, u32[]{:S(2)}) copy-start(bf16[768,768]{1,0:T(8,128)(2,1)} %all-gather.18.cloned.1.call-done) | copy-start | bytes 3538948
  323.3 11.5 copy-start.6
  364.6 21.7 %copy-start.14 = (f32[2,2,256,12,64]{2,4,3,1,0:T(8,128)S(1)}, f32[2,2,256,12,64]{2,4,3,1,0:T(8,128)}, u32[]{:S(2)}) copy-start(f32[2,2,256,12,64]{2,4,3,1,0:T(8,128)} %get-tuple-element.446) | copy-start | bytes 9437188 | tf_op jit(solution)/shard_map/while
  412.4 11.5 copy-start.6
  453.7 21.7 %copy-start.14 = (f32[2,2,256,12,64]{2,4,3,1,0:T(8,128)S(1)}, f32[2,2,256,12,64]{2,4,3,1,0:T(8,128)}, u32[]{:S(2)}) copy-start(f32[2,2,256,12,64]{2,4,3,1,0:T(8,128)} %get-tuple-element.446) | copy-start | bytes 9437188 | tf_op jit(solution)/shard_map/while
  504.6 119.9 %reduce-scatter.11.cloned.1.call-start = ((), (), s32[]{:S(2)}) async-start(), calls=%async_computation.16 | async-start | bytes 7864320 | tf_op jit(solution)/shard_map/reduce_scatter | solution.py:240
  513.4 139.9 %reduce-scatter.15.cloned.1.call-start = ((), (), s32[]{:S(2)}) async-start(), calls=%async_computation.18 | async-start | bytes 1474560 | tf_op jit(solution)/shard_map/reduce_scatter | solution.py:291
  519.9 183.9 %reduce-scatter.19.cloned.1.call-start = ((), (), s32[]{:S(2)}) async-start(), calls=%async_computation.20 | async-start | bytes 5898240 | tf_op jit(solution)/shard_map/reduce_scatter | solution.py:300
  532.5 221.6 %reduce-scatter.17.cloned.1.call-start = ((), (), s32[]{:S(2)}) async-start(), calls=%async_computation.19 | async-start | bytes 5898240 | tf_op jit(solution)/shard_map/reduce_scatter | solution.py:294
  544.4 233.0 %reduce-scatter.23.cloned.1.call-start = ((), (), s32[]{:S(2)}) async-start(), calls=%async_computation.22 | async-start | bytes 327680 | tf_op jit(solution)/shard_map/reduce_scatter | solution.py:318
  548.7 17.8 %copy-start.25 = (f32[4,256,64]{1,2,0:T(8,128)S(1)}, f32[4,256,64]{1,2,0:T(8,128)}, u32[]{:S(2)}) copy-start(f32[4,256,64]{1,2,0:T(8,128)} %copy-done.24) | copy-start | bytes 786436
  582.9 41.6 %copy-start.35 = (f32[4,768]{1,0:T(4,128)S(1)}, f32[4,768]{1,0:T(4,128)}, u32[]{:S(2)}) copy-start(f32[4,768]{1,0:T(4,128)} %copy-done.34) | copy-start | bytes 36868
  582.9 41.6 %copy-start.41 = (f32[4,256]{1,0:T(4,128)S(1)}, f32[4,256]{1,0:T(4,128)}, u32[]{:S(2)}) copy-start(f32[4,256]{1,0:T(4,128)} %copy-done.40) | copy-start | bytes 12292
  582.9 41.6 %copy-start.43 = (f32[768]{0:T(1024)S(1)}, f32[768]{0:T(1024)}, u32[]{:S(2)}) copy-start(f32[768]{0:T(1024)} %copy-done.42) | copy-start | bytes 9220
  582.9 41.6 %copy-start.45 = (f32[4,256]{1,0:T(4,128)S(1)}, f32[4,256]{1,0:T(4,128)}, u32[]{:S(2)}) copy-start(f32[4,256]{1,0:T(4,128)} %copy-done.44) | copy-start | bytes 12292
  624.6 11.4 copy-start.61
  635.9 170.2 %reduce-scatter.21.cloned.1.call-start = ((), (), s32[]{:S(2)}) async-start(), calls=%async_computation.21 | async-start | bytes 1474560 | tf_op jit(solution)/shard_map/reduce_scatter | solution.py:306
  640.8 208.3 %reduce-scatter.13.cloned.1.call-start = ((), (), s32[]{:S(2)}) async-start(), calls=%async_computation.17 | async-start | bytes 4423680 | tf_op jit(solution)/shard_map/reduce_scatter | solution.py:288
  649.0 105.1 %copy-start.62 = (bf16[3072]{0:T(1024)(128)(2,1)S(1)}, bf16[3072]{0:T(1024)(128)(2,1)}, u32[]{:S(2)}) copy-start(bf16[3072]{0:T(1024)(128)(2,1)} %get-tuple-element.264) | copy-start | bytes 18436
  649.0 105.1 %copy-start.70 = (bf16[768]{0:T(1024)(128)(2,1)S(1)}, bf16[768]{0:T(1024)(128)(2,1)}, u32[]{:S(2)}) copy-start(bf16[768]{0:T(1024)(128)(2,1)} %get-tuple-element.160) | copy-start | bytes 4612
  764.8 84.3 %copy-start.30 = (bf16[768,768]{1,0:T(8,128)(2,1)S(1)}, bf16[768,768]{1,0:T(8,128)(2,1)}, u32[]{:S(2)}) copy-start(bf16[768,768]{1,0:T(8,128)(2,1)} %reduce-scatter.19.cloned.1.call-done) | copy-start | bytes 3538948
  764.8 84.3 %copy-start.33 = (bf16[192,768]{1,0:T(8,128)(2,1)S(1)}, bf16[192,768]{1,0:T(8,128)(2,1)}, u32[]{:S(2)}) copy-start(bf16[192,768]{1,0:T(8,128)(2,1)} %reduce-scatter.15.cloned.1.call-done) | copy-start | bytes 884740
  764.8 390.7 %copy-start.1 = (bf16[1024,128]{1,0:T(8,128)(2,1)S(1)}, bf16[1024,128]{1,0:T(8,128)(2,1)}, u32[]{:S(2)}) copy-start(bf16[1024,128]{1,0:T(8,128)(2,1)} %param.20) | copy-start | bytes 786436
  (48 other events, 245.8 us)
Sparse Core Ops, SparseCore 0:
  9.6 20.2 all-gather.9
  31.5 30.7 all-gather.11
  73.6 46.4 all-gather.13
  122.1 46.3 all-gather.15
  169.9 17.4 all-gather.17
  188.8 37.4 all-gather.19
  227.9 37.4 all-gather.21
  504.8 58.6 reduce-scatter.8
  566.1 58.3 reduce-scatter.10
  627.5 25.7 reduce-scatter.14
  656.0 47.8 reduce-scatter.18
  706.2 47.8 reduce-scatter.16
  757.3 20.0 reduce-scatter.22
  780.3 25.7 reduce-scatter.20
  808.7 40.4 reduce-scatter.12
where the time goes:
time: 1170 us; the launch traced here: 1160 us
  blocking collectives  336 us (29%)
  waiting for transfers between devices  302 us (26%)
  matrix products  279 us (24%)
  local copies, waits for them, and re-layouts  113 us (10%)
  other arithmetic  113 us (10%)
  between operations  17.8 us (2%)
    psum x1, blocking collectives, shards(): lax.psum((shares[0], shares[1], shares[2], shares[3], shares[4], shares[5...  306 us
    reduce_scatter x1, waiting for transfers between devices, shards(): lax.psum_scatter(terms[4].astype(jnp.bfloat16), 'seq', scatter_dimension=...  50.5 us
    reduce_scatter x1, waiting for transfers between devices, shards(): lax.psum_scatter(terms[2].astype(jnp.bfloat16), 'seq', scatter_dimension=...  50.3 us
    convert_element_type x2, other arithmetic, attend_back(): scores_grad = (probs * (probs_grad - center)).astype(low_type)  43.4 us
    reduce_scatter x1, waiting for transfers between devices, shards(): lax.psum_scatter(terms[0].astype(jnp.bfloat16), 'seq', scatter_dimension=...  43 us
    all_gather x1, waiting for transfers between devices, shards(): lax.all_gather(keys_local, 'seq', axis=1, tiled=True)  37.9 us
    dot_general x2, matrix products, attend_back(): jnp.einsum('gqhd,gkhd->ghqk', mixed_grad_b, values_h, preferred_element_t...  35.2 us
    reduce_scatter x1, waiting for transfers between devices, shards(): lax.psum_scatter(values_term.reshape(seqs, length, width).astype(jnp.bflo...  34.6 us
  transfers between devices with their start and end apart: 15, of which 10 were waited for; matrix products, arithmetic and copies ran while one was open for 22% of the time, Pallas kernels for 0%

commit v1 on v0

--- a/solution.py
+++ b/solution.py
@@ -7,6 +7,26 @@
 
 HEADS = 12
 EPSILON = 1e-05
+
+
+def do_pairs_all_up(x0):
+    row_axis = "seq"
+    state_next, left_arr, new = (lax.axis_size(row_axis), lax.axis_index(row_axis), x0.shape[0])
+    z, last = (x0, 1)
+    while last < state_next:
+        z = jnp.concatenate(
+            [
+                z,
+                lax.ppermute(
+                    z,
+                    axis_name=row_axis,
+                    perm=list(map(lambda i0: (i0, (i0 - last) % state_next), range(state_next))),
+                ),
+            ],
+            axis=0,
+        )
+        last = 2 * last
+    return jnp.roll(z, left_arr * new, axis=0)
 
 
 def rotate_half(values):
@@ -69,7 +89,7 @@
     head_width = width // HEADS
     scale = 1.0 / math.sqrt(head_width)
     gathered = (
-        lax.all_gather(heads_weight, "seq", axis=0, tiled=True),
+        do_pairs_all_up(heads_weight),
         lax.all_gather(merge_weight, "seq", axis=0, tiled=True),
         lax.all_gather(lift_weight, "seq", axis=0, tiled=True),
         lax.all_gather(lift_bias, "seq", axis=0, tiled=True),

time: 1170 us -> 1190 us (1.017)
    ppermute x0 -> x2, waiting for transfers between devices: none -> 36.4 us  [do_pairs_all_up(): lax.ppermute(z, axis_name=row_axis, perm=list(map(lambda i0: (i0, (i0 - l...]
    all_gather x1 -> x0, waiting for transfers between devices: 29.1 us -> none  [shards(): lax.all_gather(heads_weight, 'seq', axis=0, tiled=True)]
  transfers between devices with their start and end apart: 15 -> 16, of which waited for: 10 -> 10; matrix products, arithmetic and copies ran while one was open for 22% -> 21% of each run, Pallas kernels for 0% -> 0%
where the time goes in v1:
time: 1190 us; the launch traced here: 1180 us
  blocking collectives  338 us (28%)
  waiting for transfers between devices  309 us (26%)
  matrix products  279 us (23%)
  local copies, waits for them, and re-layouts  119 us (10%)
  other arithmetic  115 us (10%)
  between operations  18 us (2%)
    psum x1, blocking collectives, shards(): lax.psum((shares[0], shares[1], shares[2], shares[3], shares[4], shares[5...  306 us
    reduce_scatter x1, waiting for transfers between devices, shards(): lax.psum_scatter(terms[2].astype(jnp.bfloat16), 'seq', scatter_dimension=...  50.5 us
    reduce_scatter x1, waiting for transfers between devices, shards(): lax.psum_scatter(terms[4].astype(jnp.bfloat16), 'seq', scatter_dimension=...  50.4 us
    convert_element_type x2, other arithmetic, attend_back(): scores_grad = (probs * (probs_grad - center)).astype(low_type)  43.4 us
    reduce_scatter x1, waiting for transfers between devices, shards(): lax.psum_scatter(terms[0].astype(jnp.bfloat16), 'seq', scatter_dimension=...  43 us
    all_gather x1, waiting for transfers between devices, shards(): lax.all_gather(keys_local, 'seq', axis=1, tiled=True)  38.4 us
    ppermute x2, waiting for transfers between devices, do_pairs_all_up(): lax.ppermute(z, axis_name=row_axis, perm=list(map(lambda i0: (i0, (i0 - l...  36.4 us
    dot_general x2, matrix products, attend_back(): jnp.einsum('gqhd,gkhd->ghqk', mixed_grad_b, values_h, preferred_element_t...  35.2 us
  transfers between devices with their start and end apart: 16, of which 10 were waited for; matrix products, arithmetic and copies ran while one was open for 21% of the time, Pallas kernels for 0%

profile of v1, /device:TPU:0, one launch (start us, length us, event | category | flops | bytes accessed | tf_op | source)
XLA Modules:
  0.0 1182.5 jit_solution(12861678087886881850)
XLA Ops:
  15.5 10.5 all-reduce.10
  37.3 36.4 %collective-permute-done.1 = bf16[384,2304]{1,0:T(8,128)(2,1)} collective-permute-done((bf16[384,2304]{1,0:T(8,128)(2,1)}, bf16[384,2304]{1,0:T(8,128)(2,1)}, u32[]{:S(2)}, u32[]{:S(2)}) %collective-permute-start.1) | collective-permute-done | bytes 1769504 | tf_op jit(solution)/shard_map/ppermute | solution.py:20
  81.5 6.3 fusion.52
  115.4 6.6 add_convert_fusion.2
  126.4 5.7 all-gather.1
  141.3 8.8 copy.93
  150.0 38.4 %all-gather.13.cloned.1.call-done = bf16[4,1024,768]{2,1,0:T(8,128)(2,1)} async-done(((bf16[4,256,768]{2,1,0:T(8,128)(2,1)}), bf16[4,1024,768]{2,1,0:T(8,128)(2,1)}) %all-gather.13.cloned.1.call-update) | async-done | bytes 6291472 | tf_op jit(solution)/shard_map/all_gather | solution.py:136
  188.5 8.7 copy.94
  197.2 74.9 %while.28 = (s32[]{:T(128)}, bf16[2,2,256,12,64]{2,4,3,1,0:T(8,128)(2,1)}, f32[2,2,12,256]{3,2,1,0:T(8,128)S(1)}, bf16[2,2,1024,768]{2,3,1,0:T(8,128)(2,1)}, bf1...) while((s32[]{:T(128)}, bf16[2,2,256,12,64]{2,4,3,1,0:T(8,128)(2,1)}, ...), condition=%wide.region_5.6_spmd.clone, body=%wide.region_2.5_spmd.sunk.clone | while | flops 1667229696 | bytes 96952408 | solution.py:160
  200.8 10.2 multiply_reduce_fusion.11
  211.1 11.6 fusion.147
  222.7 11.8 bitcast_dynamic-update-slice_fusion.9
  238.2 10.3 multiply_reduce_fusion.11
  248.5 11.8 fusion.147
  260.3 11.8 bitcast_dynamic-update-slice_fusion.9
  279.4 11.3 fusion.40
  290.7 16.6 %fusion.97 = (bf16[3072]{0:T(1024)(128)(2,1)}, bf16[4,256,3072]{2,1,0:T(8,128)(2,1)}) fusion(f32[4,256,3072]{2,1,0:T(8,128)} %fusion.40, f32[3072]{0:T(1024)S(1)} %bitcast.210, bf16[3072,768]{1,0:T(8,128)(2,1)} %all-gather.19.cloned.1.call-done, bf16[4,256,768]{2,1,0:T(8,128)(2,1)S(1)} %copy-done.28, f32[4,768]{1,0:T(4,128)S(1)} %copy-done.37), kind=kOutput, calls=%fused_computation.185 | convolution fusion | flops 4903400448 | bytes 25196544 | tf_op jit(solution)/shard_map/scd,fd->scf/dot_general | solution.py:184
  307.3 10.2 multiply_reduce_fusion.2
  317.5 15.1 %fusion.67 = (f32[4,768]{1,0:T(4,128)}, bf16[4,256,768]{2,1,0:T(8,128)(2,1)}, f32[4,768]{1,0:T(4,128)}, f32[4,256,768]{2,1,0:T(8,128)S(1)}) fusion(bf16[4,256,768]{2,1,0:T(8,128)(2,1)S(1)} %copy-done.28, f32[768]{0:T(1024)S(1)} %copy-done.66, f32[4,256,768]{2,1,0:T(8,128)S(1)} %copy-done.18, f32[4,768]{1,0:T(4,128)S(1)} %copy-done.37, ...), kind=kOutput, calls=%fused_computation.96 | convolution fusion | flops 4877445120 | bytes 33114112 | tf_op jit(solution)/shard_map/scf,fd->scd/dot_general | solution.py:173
  337.3 178.3 %while.29 = (s32[]{:T(128)}, f32[2,2,256,12,64]{2,4,3,1,0:T(8,128)}, bf16[2,2,1024,768]{2,3,1,0:T(8,128)(2,1)}, bf16[2,2,1024,768]{2,3,1,0:T(8,128)(2,1)}, bf16[...) while((s32[]{:T(128)}, ...), condition=%wide.region_12.13_spmd.clone, body=%wide.region_10.12_spmd.sunk.clone | while | flops 4105562112 | bytes 316326176 | solution.py:243
  343.5 11.4 fusion.157
  354.9 12.2 %fusion.158 = bf16[2,12,64,1024]{3,2,1,0:T(8,128)(2,1)} fusion(f32[2,12,256,1024]{3,2,1,0:T(8,128)} %fusion.157, f32[2,12,256]{2,1,0:T(8,128)S(1)} %dynamic-slice_bitcast_fusion.3, bf16[2,2,256,12,64]{2,4,3,1,0:T(8,128)(2,1)S(1)} %copy-done.6, s32[]{:T(128)S(6)} %copy.140), kind=kOutput, calls=%fused_computation.18.clone.1.clone | convolution fusion | flops 824180736 | bytes 29130756 | tf_op jit(solution)/shard_map/while/body/eval_jaxpr/ghqk,gqhd->gkhd/dot_general | solution.py:220
  367.1 17.6 %multiply_reduce_fusion.12 = (f32[2,12,256]{2,1,0:T(8,128)S(1)}, f32[2,12,256,1024]{3,2,1,0:T(8,128)}) fusion(f32[2,12,256,1024]{3,2,1,0:T(8,128)} %fusion.157, f32[2,12,256]{2,1,0:T(8,128)S(1)} %dynamic-slice_bitcast_fusion.3, bf16[2,1024,12,64]{1,3,2,0:T(8,128)(2,1)} %bitcast.188, bf16[2,2,256,12,64]{2,4,3,1,0:T(8,128)(2,1)} %get-tuple-element.461, ...), kind=kOutput, calls=%fused_computation.15.clone.1.clone | convolution fusion | flops 830466048 | bytes 54312964 | tf_op jit(solution)/shard_map/while/body/eval_jaxpr/gqhd,gkhd->ghqk/dot_general | solution.py:223
  384.7 21.7 %multiply_convert_fusion.9 = bf16[2,12,256,1024]{3,2,1,0:T(8,128)(2,1)} fusion(f32[2,12,256,1024]{3,2,1,0:T(8,128)} %get-tuple-element.404, f32[2,12,256,1024]{3,2,1,0:T(8,128)} %fusion.157, f32[2,12,256]{2,1,0:T(8,128)S(1)} %get-tuple-element.405, f32[2,12,256]{2,1,0:T(8,128)S(1)} %dynamic-slice_bitcast_fusion.3), kind=kLoop, calls=%fused_computation.14.clone.1.clone | loop fusion | flops 31457280 | bytes 62963712 | tf_op jit(solution)/shard_map/while/body/eval_jaxpr/convert_element_type | solution.py:227
  406.4 8.5 bitcast_dynamic-update-slice_fusion.11
  414.9 8.3 broadcast_multiply_fusion.12
  432.4 11.4 fusion.157
  443.8 12.2 %fusion.158 = bf16[2,12,64,1024]{3,2,1,0:T(8,128)(2,1)} fusion(f32[2,12,256,1024]{3,2,1,0:T(8,128)} %fusion.157, f32[2,12,256]{2,1,0:T(8,128)S(1)} %dynamic-slice_bitcast_fusion.3, bf16[2,2,256,12,64]{2,4,3,1,0:T(8,128)(2,1)S(1)} %copy-done.6, s32[]{:T(128)S(6)} %copy.140), kind=kOutput, calls=%fused_computation.18.clone.1.clone | convolution fusion | flops 824180736 | bytes 29130756 | tf_op jit(solution)/shard_map/while/body/eval_jaxpr/ghqk,gqhd->gkhd/dot_general | solution.py:220
  456.0 17.6 %multiply_reduce_fusion.12 = (f32[2,12,256]{2,1,0:T(8,128)S(1)}, f32[2,12,256,1024]{3,2,1,0:T(8,128)}) fusion(f32[2,12,256,1024]{3,2,1,0:T(8,128)} %fusion.157, f32[2,12,256]{2,1,0:T(8,128)S(1)} %dynamic-slice_bitcast_fusion.3, bf16[2,1024,12,64]{1,3,2,0:T(8,128)(2,1)} %bitcast.188, bf16[2,2,256,12,64]{2,4,3,1,0:T(8,128)(2,1)} %get-tuple-element.461, ...), kind=kOutput, calls=%fused_computation.15.clone.1.clone | convolution fusion | flops 830466048 | bytes 54312964 | tf_op jit(solution)/shard_map/while/body/eval_jaxpr/gqhd,gkhd->ghqk/dot_general | solution.py:223
  473.6 21.7 %multiply_convert_fusion.9 = bf16[2,12,256,1024]{3,2,1,0:T(8,128)(2,1)} fusion(f32[2,12,256,1024]{3,2,1,0:T(8,128)} %get-tuple-element.404, f32[2,12,256,1024]{3,2,1,0:T(8,128)} %fusion.157, f32[2,12,256]{2,1,0:T(8,128)S(1)} %get-tuple-element.405, f32[2,12,256]{2,1,0:T(8,128)S(1)} %dynamic-slice_bitcast_fusion.3), kind=kLoop, calls=%fused_computation.14.clone.1.clone | loop fusion | flops 31457280 | bytes 62963712 | tf_op jit(solution)/shard_map/while/body/eval_jaxpr/convert_element_type | solution.py:227
  495.3 8.5 bitcast_dynamic-update-slice_fusion.11
  503.8 8.3 broadcast_multiply_fusion.12
  515.6 8.7 copy.102
  524.4 8.7 copy.106
  539.7 12.5 %bitcast_convert_fusion = bf16[3072,768]{1,0:T(8,128)(2,1)} fusion(bf16[4,256,768]{2,1,0:T(8,128)(2,1)S(1)} %copy-done.29, f32[4,768]{1,0:T(4,128)S(1)} %copy-done.38, f32[4,256,3072]{2,1,0:T(8,128)} %fusion.40, f32[3072]{0:T(1024)S(1)} %bitcast.212), kind=kOutput, calls=%fused_computation.53 | convolution fusion | flops 4868014080 | bytes 18898944 | tf_op jit(solution)/shard_map/scf,scd->fd/dot_general | solution.py:180
  554.1 10.0 bitcast_convert_fusion.1
  568.4 14.9 %reduce-scatter.9.cloned.1.call-done = bf16[4,256,768]{2,1,0:T(8,128)(2,1)} async-done(((bf16[4,1024,768]{2,1,0:T(8,128)(2,1)}), bf16[4,256,768]{2,1,0:T(8,128)(2,1)}) %reduce-scatter.9.cloned.1.call-update) | async-done | bytes 1572880 | tf_op jit(solution)/shard_map/reduce_scatter | solution.py:254
  602.8 7.0 subtract_convert_fusion.1
  609.7 34.7 %reduce-scatter.11.cloned.1.call-done = bf16[4,256,768]{2,1,0:T(8,128)(2,1)} async-done(((bf16[4,1024,768]{2,1,0:T(8,128)(2,1)}), bf16[4,256,768]{2,1,0:T(8,128)(2,1)}) %reduce-scatter.11.cloned.1.call-update) | async-done | bytes 1572880 | tf_op jit(solution)/shard_map/reduce_scatter | solution.py:260
  644.5 9.4 fusion.64
  661.2 7.9 bitcast_convert_fusion.2
  673.3 50.4 %reduce-scatter.19.cloned.1.call-done = bf16[768,768]{1,0:T(8,128)(2,1)} async-done(((bf16[3072,768]{1,0:T(8,128)(2,1)}), bf16[768,768]{1,0:T(8,128)(2,1)}) %reduce-scatter.19.cloned.1.call-update) | async-done | bytes 1179664 | tf_op jit(solution)/shard_map/reduce_scatter | solution.py:320
  723.7 50.5 %reduce-scatter.17.cloned.1.call-done = bf16[192,3072]{1,0:T(8,128)(2,1)} async-done(((bf16[768,3072]{1,0:T(8,128)(2,1)}), bf16[192,3072]{1,0:T(8,128)(2,1)}) %reduce-scatter.17.cloned.1.call-update) | async-done | bytes 1179664 | tf_op jit(solution)/shard_map/reduce_scatter | solution.py:314
  774.2 10.3 all-reduce.9
  789.4 7.9 reduce-scatter.23.cloned.1.call-done
  797.3 28.9 %reduce-scatter.21.cloned.1.call-done = bf16[1152,128]{1,0:T(8,128)(2,1)} async-done(((bf16[4608,128]{1,0:T(8,128)(2,1)}), bf16[1152,128]{1,0:T(8,128)(2,1)}) %reduce-scatter.21.cloned.1.call-update) | async-done | bytes 294928 | tf_op jit(solution)/shard_map/reduce_scatter | solution.py:326
  826.2 43.0 %reduce-scatter.13.cloned.1.call-done = bf16[192,2304]{1,0:T(8,128)(2,1)} async-done(((bf16[768,2304]{1,0:T(8,128)(2,1)}), bf16[192,2304]{1,0:T(8,128)(2,1)}) %reduce-scatter.13.cloned.1.call-update) | async-done | bytes 884752 | tf_op jit(solution)/shard_map/reduce_scatter | solution.py:308
  869.2 306.4 %all-reduce.12 = (f32[192,2304]{1,0:T(8,128)}, f32[192,768]{1,0:T(8,128)}, f32[192,3072]{1,0:T(8,128)}, f32[768]{0:T(1024)}, f32[768,768]{1,0:T(8,128)}, /*index...) all-reduce(bf16[192,2304]{1,0:T(8,128)(2,1)} %reduce-scatter.13.clo, ...), channel_id=1, replica_groups=mesh['dp'=8,'seq'=4] {'dp'}, use_global_device_ids=true, to_apply=%region_18.19 | all-reduce | flops 1952192 | bytes 11718144 | tf_op jit(solution)/shard_map/psum | solution.py:342
  (312 shorter events, 151.2 us)
Async XLA Ops:
  7.2 25.6 %copy-start = (bf16[1024,128]{1,0:T(8,128)(2,1)S(1)}, bf16[1024,128]{1,0:T(8,128)(2,1)}, u32[]{:S(2)}) copy-start(bf16[1024,128]{1,0:T(8,128)(2,1)} %param.20) | copy-start | bytes 786436
  7.2 24.1 %copy-start.20 = (bf16[192,2304]{1,0:T(8,128)(2,1)S(1)}, bf16[192,2304]{1,0:T(8,128)(2,1)}, u32[]{:S(2)}) copy-start(bf16[192,2304]{1,0:T(8,128)(2,1)} %param.23) | copy-start | bytes 2654212
  7.2 18.8 %copy-start.67 = (bf16[1152]{0:T(1024)(128)(2,1)S(1)}, bf16[1152]{0:T(1024)(128)(2,1)}, u32[]{:S(2)}) copy-start(bf16[1152]{0:T(1024)(128)(2,1)} %param.30) | copy-start | bytes 6916
  7.3 27.8 %all-gather.9.cloned.1.call-start = ((), (), s32[]{:S(2)}) async-start(), calls=%async_computation.8 | async-start | bytes 1474560 | tf_op jit(solution)/shard_map/all_gather | solution.py:98
  7.3 24.0 %collective-permute-start = (bf16[192,2304]{1,0:T(8,128)(2,1)}, bf16[192,2304]{1,0:T(8,128)(2,1)S(1)}, u32[]{:S(2)}, u32[]{:S(2)}) collective-permute-start(bf16[192,2304]{1,0:T(8,128)(2,1)} %param.23), channel_id=1, source_target_pairs={{0,3},{1,0},{2,1},{3,2},{4,7},{5,4},{6,5},{7,6},{8,11},{9,8},{10,9... | collective-permute-start | bytes 2654216 | tf_op jit(solution)/shard_map/ppermute | solution.py:20
  9.8 23.1 %copy-start.74 = (s32[4]{0:T(128)S(1)}, s32[4]{0:T(128)}, u32[]{:S(2)}) copy-start(s32[4]{0:T(128)} %param.21) | copy-start | bytes 52
  9.8 131.5 %all-gather.11.cloned.1.call-start = ((), (), s32[]{:S(2)}) async-start(), calls=%async_computation.9 | async-start | bytes 7864320 | tf_op jit(solution)/shard_map/all_gather | solution.py:137
  11.5 70.0 %copy-start.41 = (f32[4,256]{1,0:T(4,128)}, f32[4,256]{1,0:T(4,128)S(1)}, u32[]{:S(2)}) copy-start(f32[4,256]{1,0:T(4,128)S(1)} %broadcast_multiply_fusion.9) | copy-start | bytes 12292
  26.1 55.4 %copy-start.43 = (f32[768]{0:T(1024)}, f32[768]{0:T(1024)S(1)}, u32[]{:S(2)}) copy-start(f32[768]{0:T(1024)S(1)} %convert_element_type.165) | copy-start | bytes 9220
  32.6 41.1 %collective-permute-start.1 = (bf16[384,2304]{1,0:T(8,128)(2,1)}, bf16[384,2304]{1,0:T(8,128)(2,1)}, u32[]{:S(2)}, u32[]{:S(2)}) collective-permute-start(bf16[384,2304]{1,0:T(8,128)(2,1)} %pad_maximum_fusion.5), channel_id=1, source_target_pairs={{0,2},{1,3},{2,0},{3,1},{4,6},{5,7},{6,4},{7,5},{8,10},{9,11},{10,... | collective-permute-start | bytes 5308424 | tf_op jit(solution)/shard_map/ppermute | solution.py:20
  32.8 48.6 %copy-start.45 = (f32[4,256]{1,0:T(4,128)}, f32[4,256]{1,0:T(4,128)S(1)}, u32[]{:S(2)}) copy-start(f32[4,256]{1,0:T(4,128)S(1)} %add_rsqrt_fusion.1) | copy-start | bytes 12292
  37.3 44.2 %copy-start.35 = (f32[4,768]{1,0:T(4,128)}, f32[4,768]{1,0:T(4,128)S(1)}, u32[]{:S(2)}) copy-start(f32[4,768]{1,0:T(4,128)S(1)} %get-tuple-element.257) | copy-start | bytes 36868
  37.3 44.2 %copy-start.49 = (f32[4,768]{1,0:T(4,128)}, f32[4,768]{1,0:T(4,128)S(1)}, u32[]{:S(2)}) copy-start(f32[4,768]{1,0:T(4,128)S(1)} %get-tuple-element.256) | copy-start | bytes 36868
  92.8 95.7 %all-gather.13.cloned.1.call-start = ((), (), s32[]{:S(2)}) async-start(), calls=%async_computation.10 | async-start | bytes 7864320 | tf_op jit(solution)/shard_map/all_gather | solution.py:136
  94.0 15.9 %copy-start.25 = (f32[4,256,64]{1,2,0:T(8,128)}, f32[4,256,64]{1,2,0:T(8,128)S(1)}, u32[]{:S(2)}) copy-start(f32[4,256,64]{1,2,0:T(8,128)S(1)} %get-tuple-element.250) | copy-start | bytes 786436
  98.5 16.9 %copy-start.8 = (f32[4,256,768]{2,1,0:T(8,128)}, f32[4,256,768]{2,1,0:T(8,128)S(1)}, u32[]{:S(2)}) copy-start(f32[4,256,768]{2,1,0:T(8,128)S(1)} %copy.90) | copy-start | bytes 9437188
  122.0 150.1 %all-gather.15.cloned.1.call-start = ((), (), s32[]{:S(2)}) async-start(), calls=%async_computation.11 | async-start | bytes 1474560 | tf_op jit(solution)/shard_map/all_gather | solution.py:93
  122.6 156.7 %all-gather.17.cloned.1.call-start = ((), (), s32[]{:S(2)}) async-start(), calls=%async_computation.12 | async-start | bytes 5898240 | tf_op jit(solution)/shard_map/all_gather | solution.py:94
  123.2 167.5 %all-gather.19.cloned.1.call-start = ((), (), s32[]{:S(2)}) async-start(), calls=%async_computation.13 | async-start | bytes 5898240 | tf_op jit(solution)/shard_map/all_gather | solution.py:96
  123.8 459.5 %reduce-scatter.9.cloned.1.call-start = ((), (), s32[]{:S(2)}) async-start(), calls=%async_computation.14 | async-start | bytes 7864320 | tf_op jit(solution)/shard_map/reduce_scatter | solution.py:254
  197.2 74.9 %copy-start.11 = (bf16[4,256,768]{2,1,0:T(8,128)(2,1)S(1)}, bf16[4,256,768]{2,1,0:T(8,128)(2,1)}, u32[]{:S(2)}) copy-start(bf16[4,256,768]{2,1,0:T(8,128)(2,1)} %param.19) | copy-start | bytes 4718596
  197.2 74.9 %copy-start.39 = (f32[4,768]{1,0:T(4,128)S(1)}, f32[4,768]{1,0:T(4,128)}, u32[]{:S(2)}) copy-start(f32[4,768]{1,0:T(4,128)} %get-tuple-element.258) | copy-start | bytes 36868
  277.2 40.3 %copy-start.47 = (f32[4,256]{1,0:T(4,128)}, f32[4,256]{1,0:T(4,128)S(1)}, u32[]{:S(2)}) copy-start(f32[4,256]{1,0:T(4,128)S(1)} %broadcast_multiply_fusion.8) | copy-start | bytes 12292
  279.3 38.2 %copy-start.69 = (f32[4,256]{1,0:T(4,128)}, f32[4,256]{1,0:T(4,128)S(1)}, u32[]{:S(2)}) copy-start(f32[4,256]{1,0:T(4,128)S(1)} %add_rsqrt_fusion) | copy-start | bytes 12292
  290.7 16.6 %copy-start.18 = (f32[4,256,768]{2,1,0:T(8,128)S(1)}, f32[4,256,768]{2,1,0:T(8,128)}, u32[]{:S(2)}) copy-start(f32[4,256,768]{2,1,0:T(8,128)} %copy-done.17) | copy-start | bytes 9437188
  290.7 16.6 %copy-start.76 = (bf16[768,3072]{1,0:T(8,128)(2,1)S(1)}, bf16[768,3072]{1,0:T(8,128)(2,1)}, u32[]{:S(2)}) copy-start(bf16[768,3072]{1,0:T(8,128)(2,1)} %all-gather.17.cloned.1.call-done) | copy-start | bytes 14155780
  317.5 16.8 %copy-start.32 = (bf16[768,768]{1,0:T(8,128)(2,1)S(1)}, bf16[768,768]{1,0:T(8,128)(2,1)}, u32[]{:S(2)}) copy-start(bf16[768,768]{1,0:T(8,128)(2,1)} %all-gather.15.cloned.1.call-done) | copy-start | bytes 3538948
  343.5 11.5 copy-start.6
  384.7 21.7 %copy-start.14 = (f32[2,2,256,12,64]{2,4,3,1,0:T(8,128)S(1)}, f32[2,2,256,12,64]{2,4,3,1,0:T(8,128)}, u32[]{:S(2)}) copy-start(f32[2,2,256,12,64]{2,4,3,1,0:T(8,128)} %get-tuple-element.446) | copy-start | bytes 9437188 | tf_op jit(solution)/shard_map/while
  473.6 21.7 %copy-start.14 = (f32[2,2,256,12,64]{2,4,3,1,0:T(8,128)S(1)}, f32[2,2,256,12,64]{2,4,3,1,0:T(8,128)}, u32[]{:S(2)}) copy-start(f32[2,2,256,12,64]{2,4,3,1,0:T(8,128)} %get-tuple-element.446) | copy-start | bytes 9437188 | tf_op jit(solution)/shard_map/while
  524.3 120.1 %reduce-scatter.11.cloned.1.call-start = ((), (), s32[]{:S(2)}) async-start(), calls=%async_computation.15 | async-start | bytes 7864320 | tf_op jit(solution)/shard_map/reduce_scatter | solution.py:260
  533.2 140.1 %reduce-scatter.15.cloned.1.call-start = ((), (), s32[]{:S(2)}) async-start(), calls=%async_computation.17 | async-start | bytes 1474560 | tf_op jit(solution)/shard_map/reduce_scatter | solution.py:311
  539.7 184.0 %reduce-scatter.19.cloned.1.call-start = ((), (), s32[]{:S(2)}) async-start(), calls=%async_computation.19 | async-start | bytes 5898240 | tf_op jit(solution)/shard_map/reduce_scatter | solution.py:320
  552.3 221.9 %reduce-scatter.17.cloned.1.call-start = ((), (), s32[]{:S(2)}) async-start(), calls=%async_computation.18 | async-start | bytes 5898240 | tf_op jit(solution)/shard_map/reduce_scatter | solution.py:314
  564.1 233.2 %reduce-scatter.23.cloned.1.call-start = ((), (), s32[]{:S(2)}) async-start(), calls=%async_computation.21 | async-start | bytes 327680 | tf_op jit(solution)/shard_map/reduce_scatter | solution.py:338
  568.4 18.1 %copy-start.26 = (f32[4,256,64]{1,2,0:T(8,128)S(1)}, f32[4,256,64]{1,2,0:T(8,128)}, u32[]{:S(2)}) copy-start(f32[4,256,64]{1,2,0:T(8,128)} %copy-done.25) | copy-start | bytes 786436
  602.7 41.7 %copy-start.36 = (f32[4,768]{1,0:T(4,128)S(1)}, f32[4,768]{1,0:T(4,128)}, u32[]{:S(2)}) copy-start(f32[4,768]{1,0:T(4,128)} %copy-done.35) | copy-start | bytes 36868
  602.7 41.7 %copy-start.42 = (f32[4,256]{1,0:T(4,128)S(1)}, f32[4,256]{1,0:T(4,128)}, u32[]{:S(2)}) copy-start(f32[4,256]{1,0:T(4,128)} %copy-done.41) | copy-start | bytes 12292
  602.7 41.7 %copy-start.44 = (f32[768]{0:T(1024)S(1)}, f32[768]{0:T(1024)}, u32[]{:S(2)}) copy-start(f32[768]{0:T(1024)} %copy-done.43) | copy-start | bytes 9220
  602.8 41.6 %copy-start.46 = (f32[4,256]{1,0:T(4,128)S(1)}, f32[4,256]{1,0:T(4,128)}, u32[]{:S(2)}) copy-start(f32[4,256]{1,0:T(4,128)} %copy-done.45) | copy-start | bytes 12292
  644.5 11.8 copy-start.62
  656.0 170.1 %reduce-scatter.21.cloned.1.call-start = ((), (), s32[]{:S(2)}) async-start(), calls=%async_computation.20 | async-start | bytes 1474560 | tf_op jit(solution)/shard_map/reduce_scatter | solution.py:326
  661.2 208.0 %reduce-scatter.13.cloned.1.call-start = ((), (), s32[]{:S(2)}) async-start(), calls=%async_computation.16 | async-start | bytes 4423680 | tf_op jit(solution)/shard_map/reduce_scatter | solution.py:308
  669.1 105.1 %copy-start.63 = (bf16[3072]{0:T(1024)(128)(2,1)S(1)}, bf16[3072]{0:T(1024)(128)(2,1)}, u32[]{:S(2)}) copy-start(bf16[3072]{0:T(1024)(128)(2,1)} %get-tuple-element.264) | copy-start | bytes 18436
  669.1 105.1 %copy-start.73 = (bf16[768]{0:T(1024)(128)(2,1)S(1)}, bf16[768]{0:T(1024)(128)(2,1)}, u32[]{:S(2)}) copy-start(bf16[768]{0:T(1024)(128)(2,1)} %get-tuple-element.160) | copy-start | bytes 4612
  784.9 84.3 %copy-start.31 = (bf16[768,768]{1,0:T(8,128)(2,1)S(1)}, bf16[768,768]{1,0:T(8,128)(2,1)}, u32[]{:S(2)}) copy-start(bf16[768,768]{1,0:T(8,128)(2,1)} %reduce-scatter.19.cloned.1.call-done) | copy-start | bytes 3538948
  784.9 84.3 %copy-start.34 = (bf16[192,768]{1,0:T(8,128)(2,1)S(1)}, bf16[192,768]{1,0:T(8,128)(2,1)}, u32[]{:S(2)}) copy-start(bf16[192,768]{1,0:T(8,128)(2,1)} %reduce-scatter.15.cloned.1.call-done) | copy-start | bytes 884740
  784.9 390.7 %copy-start.1 = (bf16[1024,128]{1,0:T(8,128)(2,1)S(1)}, bf16[1024,128]{1,0:T(8,128)(2,1)}, u32[]{:S(2)}) copy-start(bf16[1024,128]{1,0:T(8,128)(2,1)} %param.20) | copy-start | bytes 786436
  (55 other events, 306.0 us)
Sparse Core Ops, SparseCore 0:
  9.9 20.0 all-gather.8
  92.9 46.9 all-gather.10
  142.1 46.3 all-gather.12
  189.9 17.4 all-gather.14
  208.8 37.4 all-gather.16
  247.7 37.4 all-gather.18
  524.4 58.7 reduce-scatter.8
  586.0 58.3 reduce-scatter.10
  647.5 25.7 reduce-scatter.14
  675.8 47.8 reduce-scatter.18
  726.2 47.8 reduce-scatter.16
  777.2 20.0 reduce-scatter.22
  800.4 25.6 reduce-scatter.20
  828.7 40.4 reduce-scatter.12
